TPU v7x, 32 devices: a whole 2x2x4 slice. The times are simulated.
32 devices in a mesh: mock: 4 (over y, core), row: 8 (over z, x).
Axes of the slice: x: 2, y: 2, z: 4, core: 2. Of those that a mesh axis runs over, the one named last changes fastest.
Arguments:
- mock_maps: float32 [128, 4, 4096], P('mock', None, 'row'), parts along dimension 0, may hold values from -6 to 6
- pixel_order: int32 [4, 4096], P(None, 'row'), may hold values from 0 to 4095, as said below
- prior_solution: bfloat16 [128, 4096], P('mock', 'row'), parts along dimension 0, may hold values from -6 to 6
- factor_rows: bfloat16 [4, 4096, 3, 256], P(None, 'row'), may hold values from -0.109375 to 0.109375
- tile_columns: int32 [4, 16, 3], replicated, may hold values from 0 to 63, as said below
- panel_inverse: bfloat16 [4, 4096, 4096], P(None, 'row'), as said below
Outputs:
- whitened: float32 [128, 4, 4096], P('mock', None, 'row'), parts along dimension 0
There are 4 independent parts, one for each index of `mock`. A program takes and returns all parts, laid end to end along the dimension named above; an argument that names none is the same for every part. Nothing has to cross between parts.
Inputs may be any that keep to these rules, and one draw needn't show every extreme that they name: `pixel_order`: each aligned block of 512 entries of a panel is a permutation of its own indices within the panel. `tile_columns`: slot 0 of tile row j of panel p is p * 16 + j, slot 1 is p * 16 + ((j + 8) mod 16), and slot 2 is below (p + 1) * 16: tiles lie only in columns solved before the row's panel. `panel_inverse`: within each panel the matrix is lower triangular with a positive diagonal.
All inputs are finite; a program needn't handle non-finite values.
Results may differ from a plain program's by a relative error of at most 0.0036.
Values may be sent and summed in bfloat16 or wider, within the bound.
A program may use at most 128 MiB of HBM per device.

v0:
```python
import functools

import jax
import jax.numpy as jnp
from jax import lax
from jax.experimental import pallas as pl
from jax.experimental.pallas import tpu as pltpu
from jax.sharding import PartitionSpec as P

MESH = pl.DeviceIdType.MESH
NT = (((1,), (1,)), ((), ()))


def solve_kernel(
    n, tile, columns_ref, order_hbm, maps_hbm, prior_hbm, factor_hbm, inverse_hbm, out_hbm,
    order_ref, maps_ref, out_ref, map_sem, out_sem, residuals, inverse, factor, ordered, total,
    local_sem, factor_sem, inverse_sem, known_send, known_recv, res_send, res_recv, *knowns,
):
    me = lax.axis_index("row")
    panels, mocks, share = out_ref.shape
    width = knowns[0].shape[2]
    per_tile = tile // width
    pieces = share // width
    prior_pieces = prior_hbm.shape[1] // width
    rows_of = min(share, tile)

    if n & (n - 1) == 0:
        peers = [me ^ d for d in [*range(n - 1, 0, -2), *range(n - 2, 0, -2)]]
    else:
        peers = [lax.rem(me + d, n) for d in range(1, n)]

    barrier = pltpu.get_barrier_semaphore()

    @pl.loop(1, n)
    def _(d):
        pl.semaphore_signal(
            barrier, inc=1, device_id={"row": lax.rem(me + d, n)}, device_id_type=MESH
        )

    prior_copies = []
    for h in range(prior_pieces):
        prior_copies.append(
            pltpu.make_async_copy(
                prior_hbm.at[:, pl.ds(h * width, width)],
                knowns[0].at[me * prior_pieces + h],
                local_sem.at[h],
            )
        )
    factor_copies, inverse_copies = [], []
    for p in range(panels):
        factor_copies.append(
            pltpu.make_async_copy(factor_hbm.at[p], factor.at[p], factor_sem.at[p])
        )
        inverse_copies.append(
            pltpu.make_async_copy(inverse_hbm.at[p], inverse.at[p], inverse_sem.at[p])
        )
    for c in prior_copies:
        c.start()
    map_copies = [
        pltpu.make_async_copy(order_hbm, order_ref, map_sem.at[0]),
        pltpu.make_async_copy(maps_hbm, maps_ref, map_sem.at[1]),
    ]
    for c in map_copies:
        c.start()
    for p in range(panels):
        factor_copies[p].start()
        inverse_copies[p].start()

    def send_known(round_at):
        count = knowns[round_at].shape[0] // n
        block = knowns[round_at].at[pl.ds(me * count, count)]

        def to(peer):
            pltpu.make_async_remote_copy(
                src_ref=block,
                dst_ref=block,
                send_sem=known_send.at[round_at],
                recv_sem=known_recv.at[round_at],
                device_id={"row": peer},
                device_id_type=MESH,
            ).start()

        for peer in peers:
            to(peer)

    def wait_known(sem, round_at):
        count = knowns[round_at].shape[0] // n
        whole = knowns[round_at].at[pl.ds(0, (n - 1) * count)]
        pltpu.make_async_copy(whole, whole, sem).wait()

    for c in prior_copies:
        c.wait()
    pl.semaphore_wait(barrier, n - 1)
    send_known(0)

    for c in map_copies:
        c.wait()
    places = lax.broadcasted_iota(jnp.int32, (share, share), 0) + me * share
    for p in range(panels):
        chosen = jnp.where(places == order_ref[pl.ds(p, 1), :], 1.0, 0.0).astype(jnp.bfloat16)
        values = maps_ref[:, p, :]
        high = values.astype(jnp.bfloat16)
        rest = values - high.astype(jnp.float32)
        middle = rest.astype(jnp.bfloat16)
        low = (rest - middle.astype(jnp.float32)).astype(jnp.bfloat16)
        parts = jnp.concatenate([high, middle, low], axis=0)
        taken = jnp.dot(parts, chosen, preferred_element_type=jnp.float32)
        ordered[p] = (taken[:mocks] + taken[mocks : 2 * mocks]) + taken[2 * mocks :]

    def known_tile(q, at):
        return [knowns[q][at * per_tile + h] for h in range(per_tile)]

    def picked(p, column):
        chosen, low = None, 0
        for q in range(p + 1):
            tiles = knowns[q].shape[0] // per_tile
            found = known_tile(q, jnp.clip(column - low, 0, tiles - 1))
            if chosen is None:
                chosen = found
            else:
                chosen = [jnp.where(column >= low, new, old) for new, old in zip(found, chosen)]
            low += tiles
        return chosen

    panel_tiles = n * share // tile
    first_tile = me * share // tile
    for p in range(panels):

        def slot_update(j, k, parts):
            update = jnp.zeros((mocks, rows_of), jnp.float32)
            for h in range(per_tile):
                update += lax.dot_general(
                    parts[h],
                    factor[p, k, j * rows_of : (j + 1) * rows_of, h * width : (h + 1) * width],
                    NT,
                    preferred_element_type=jnp.float32,
                )
            return update

        factor_copies[p].wait()
        groups = range(share // rows_of)
        early = []
        if share >= tile:
            early = [slot_update(j, 0, known_tile(p, first_tile + j)) for j in groups]
        wait_known(known_recv.at[p], p)
        for j in groups:
            row_tile = first_tile + j
            update = early[j] if early else slot_update(j, 0, known_tile(p, row_tile))
            opposite = lax.rem(row_tile + panel_tiles // 2, panel_tiles)
            update += slot_update(j, 1, known_tile(p, opposite))
            for k in range(2, factor.shape[1]):
                update += slot_update(j, k, picked(p, columns_ref[k, p, row_tile]))
            span = slice(j * rows_of, (j + 1) * rows_of)
            residuals[p, me, :, span] = (ordered[p, :, span] - update).astype(jnp.bfloat16)

        def residual_copy(src, dst):
            return pltpu.make_async_remote_copy(
                src_ref=residuals.at[p, src],
                dst_ref=residuals.at[p, src],
                send_sem=res_send.at[p, dst],
                recv_sem=res_recv.at[p, src],
                device_id={"row": dst},
                device_id_type=MESH,
            )

        @pl.loop(0, n - 1 - me)
        def _(k):
            residual_copy(me, n - 1 - k).start()

        inverse_copies[p].wait()

        def product(src):
            return lax.dot_general(
                residuals[p, src],
                inverse[p, :, pl.ds(pl.multiple_of(src * share, share), share)],
                NT,
                preferred_element_type=jnp.float32,
            )

        total[...] = product(me)

        @pl.loop(1, me + 1)
        def _(d):
            src = me - d
            residual_copy(src, me).wait_recv()
            total[...] += product(src)

        solved = total[...]
        if p < panels - 1:
            for h in range(pieces):
                knowns[p + 1][me * pieces + h] = solved[:, h * width : (h + 1) * width].astype(
                    jnp.bfloat16
                )
            send_known(p + 1)
        out_ref[p] = solved
        pltpu.make_async_copy(out_ref.at[p], out_hbm.at[p], out_sem.at[p]).start()

    for p in range(panels):
        wait_known(known_send.at[p], p)
        pltpu.make_async_copy(out_ref.at[p], out_hbm.at[p], out_sem.at[p]).wait()

        @pl.loop(0, n - 1 - me)
        def _(k):
            dst = n - 1 - k
            pltpu.make_async_remote_copy(
                src_ref=residuals.at[p, me],
                dst_ref=residuals.at[p, me],
                send_sem=res_send.at[p, dst],
                recv_sem=res_recv.at[p, me],
                device_id={"row": dst},
                device_id_type=MESH,
            ).wait_send()


def per_device(n, mock_maps, pixel_order, prior_solution, factor_rows, tile_columns, panel_inverse):
    mocks, panels, share = mock_maps.shape
    slots, tile = factor_rows.shape[2:]
    width = min(share, tile, prior_solution.shape[1])
    prior_pieces = prior_solution.shape[1] // width
    factor_slots = jnp.transpose(factor_rows, (0, 2, 1, 3))
    columns = jnp.transpose(tile_columns, (2, 0, 1))
    known_pieces = [n * prior_pieces] + [n * share // width] * (panels - 1)
    any_spec = pl.BlockSpec(memory_space=pl.ANY)
    dma = pltpu.SemaphoreType.DMA
    out = pl.pallas_call(
        functools.partial(solve_kernel, n, tile),
        out_shape=jax.ShapeDtypeStruct((panels, mocks, share), jnp.float32),
        in_specs=[
            pl.BlockSpec(memory_space=pltpu.SMEM), any_spec, any_spec,
            any_spec, any_spec, any_spec,
        ],
        out_specs=any_spec,
        scratch_shapes=[
            pltpu.VMEM(pixel_order.shape, jnp.int32),
            pltpu.VMEM(mock_maps.shape, jnp.float32),
            pltpu.VMEM((panels, mocks, share), jnp.float32),
            dma((2,)),
            dma((panels,)),
            pltpu.VMEM((panels, n, mocks, share), jnp.bfloat16),
            pltpu.VMEM(panel_inverse.shape, jnp.bfloat16),
            pltpu.VMEM(factor_slots.shape, jnp.bfloat16),
            pltpu.VMEM((panels, mocks, share), jnp.float32),
            pltpu.VMEM((mocks, share), jnp.float32),
            dma((prior_pieces,)),
            dma((panels,)),
            dma((panels,)),
            dma((panels,)),
            dma((panels,)),
            dma((panels, n)),
            dma((panels, n)),
        ]
        + [pltpu.VMEM((count, mocks, width), jnp.bfloat16) for count in known_pieces],
        compiler_params=pltpu.CompilerParams(
            collective_id=0, has_side_effects=True, vmem_limit_bytes=60 * 1024 * 1024
        ),
    )(columns, pixel_order, mock_maps, prior_solution, factor_slots, panel_inverse)
    return jnp.transpose(out, (1, 0, 2))


def solution(mesh):
    return jax.shard_map(
        functools.partial(per_device, mesh.shape["row"]),
        mesh=mesh,
        in_specs=(
            P("mock", None, "row"),
            P(None, "row"),
            P("mock", "row"),
            P(None, "row", None, None),
            P(),
            P(None, "row", None),
        ),
        out_specs=P("mock", None, "row"),
        check_vma=False,
    )
```

profile of v0, /device:TPU:8, one launch (start us, length us, event | category | flops | bytes accessed | tf_op | source)
XLA Modules:
  0.0 62.9 jit_solution(5920218209357180922)
XLA Ops:
  0.0 61.0 %shard_map.64 = f32[4,32,512]{2,1,0:T(8,128)} custom-call(s32[3,4,16]{2,1,0:T(4,128)} %bitcast.5, s32[4,512]{1,0:T(4,128)} %order_hbm.1, f32[32,4,512]{2,1,0:T(4,128)} %maps_hbm.1, bf16[32,512]{1,0:T(8,128)(2,1)} %prior_hbm.1, bf16[4,3,512,256]{3,2,1,0:T(8,128)(2,1)} %bitcast.3, bf16[4,512,4096]{2,1,0:T(8,128)(2,1)} %inverse_hbm.1), custom_call_target="tpu_custom_call" | custom-call | tf_op jit(solution)/shard_map/pallas_call | solution.py:225
  61.0 1.8 %copy.7 = f32[32,4,512]{2,1,0:T(4,128)} copy(f32[32,4,512]{2,0,1:T(8,128)} %bitcast.4) | data formatting | bytes 524288 | tf_op jit(solution)/shard_map/transpose | solution.py:257
where the time goes:
time: 63.1 us; the launch traced here: 62.9 us
  Pallas kernels  61 us (97%)
  local copies, waits for them, and re-layouts  1.82 us (3%)
    pallas_call x1, Pallas kernels, per_device(): pl.pallas_call(functools.partial(solve_kernel, n, tile), out_shape=jax.Sh...  61 us
    transpose x1, local copies, waits for them, and re-layouts, per_device(): return jnp.transpose(out, (1, 0, 2))  1.82 us

commit v1 on v0

v1 whole, which is shorter than its diff:
```python
import functools

import jax
import jax.numpy as jnp
from jax import lax
from jax.experimental import pallas as pl
from jax.experimental.pallas import tpu as pltpu
from jax.sharding import PartitionSpec as P

MESH = pl.DeviceIdType.MESH
NT = (((1,), (1,)), ((), ()))
GROUPS = 2


def solve_kernel(
    n, tile, columns_ref, order_hbm, maps_hbm, prior_hbm, factor_hbm, inverse_hbm, out_hbm,
    order_ref, maps_ref, out_ref, map_sem, out_sem, residuals, inverse, factor, ordered, total,
    local_sem, factor_sem, inverse_sem, known_send, known_recv, res_send, res_recv, *blocks,
):
    me = lax.axis_index("row")
    panels, groups, part, share = out_ref.shape
    mocks = groups * part
    knowns = [blocks[p * groups : (p + 1) * groups] for p in range(panels)]
    width = blocks[0].shape[2]
    per_tile = tile // width
    pieces = share // width
    prior_pieces = prior_hbm.shape[1] // width
    rows_of = min(share, tile)

    if n & (n - 1) == 0:
        peers = [me ^ d for d in [*range(n - 1, 0, -2), *range(n - 2, 0, -2)]]
    else:
        peers = [lax.rem(me + d, n) for d in range(1, n)]

    barrier = pltpu.get_barrier_semaphore()

    @pl.loop(1, n)
    def _(d):
        pl.semaphore_signal(
            barrier, inc=1, device_id={"row": lax.rem(me + d, n)}, device_id_type=MESH
        )

    def mocks_of(g):
        return pl.ds(g * part, part)

    prior_copies = []
    for g in range(groups):
        for h in range(prior_pieces):
            prior_copies.append(
                pltpu.make_async_copy(
                    prior_hbm.at[mocks_of(g), pl.ds(h * width, width)],
                    knowns[0][g].at[me * prior_pieces + h],
                    local_sem.at[g, h],
                )
            )
    factor_copies, inverse_copies = [], []
    for p in range(panels):
        factor_copies.append(
            pltpu.make_async_copy(factor_hbm.at[p], factor.at[p], factor_sem.at[p])
        )
        inverse_copies.append(
            pltpu.make_async_copy(inverse_hbm.at[p], inverse.at[p], inverse_sem.at[p])
        )
    for c in prior_copies:
        c.start()
    map_copies = [
        pltpu.make_async_copy(order_hbm, order_ref, map_sem.at[0]),
        pltpu.make_async_copy(maps_hbm, maps_ref, map_sem.at[1]),
    ]
    for c in map_copies:
        c.start()
    for p in range(panels):
        factor_copies[p].start()
        inverse_copies[p].start()

    def send_known(p, g):
        count = knowns[p][g].shape[0] // n
        block = knowns[p][g].at[pl.ds(me * count, count)]
        for peer in peers:
            pltpu.make_async_remote_copy(
                src_ref=block,
                dst_ref=block,
                send_sem=known_send.at[p, g],
                recv_sem=known_recv.at[p, g],
                device_id={"row": peer},
                device_id_type=MESH,
            ).start()

    def wait_known(sem, p, g):
        count = knowns[p][g].shape[0] // n
        whole = knowns[p][g].at[pl.ds(0, (n - 1) * count)]
        pltpu.make_async_copy(whole, whole, sem.at[p, g]).wait()

    def residual_copy(p, g, src, dst):
        return pltpu.make_async_remote_copy(
            src_ref=residuals.at[p, g, src],
            dst_ref=residuals.at[p, g, src],
            send_sem=res_send.at[p, g, dst],
            recv_sem=res_recv.at[p, g, src],
            device_id={"row": dst},
            device_id_type=MESH,
        )

    for c in prior_copies:
        c.wait()
    pl.semaphore_wait(barrier, n - 1)
    for g in range(groups):
        send_known(0, g)

    for c in map_copies:
        c.wait()
    places = lax.broadcasted_iota(jnp.int32, (share, share), 0) + me * share

    def gather(p):
        chosen = jnp.where(places == order_ref[pl.ds(p, 1), :], 1.0, 0.0).astype(jnp.bfloat16)
        values = maps_ref[:, p, :]
        high = values.astype(jnp.bfloat16)
        rest = values - high.astype(jnp.float32)
        middle = rest.astype(jnp.bfloat16)
        low = (rest - middle.astype(jnp.float32)).astype(jnp.bfloat16)
        parts = jnp.concatenate([high, middle, low], axis=0)
        taken = jnp.dot(parts, chosen, preferred_element_type=jnp.float32)
        ordered[p] = (taken[:mocks] + taken[mocks : 2 * mocks]) + taken[2 * mocks :]

    gather(0)

    def known_tile(q, g, at):
        return [knowns[q][g][at * per_tile + h] for h in range(per_tile)]

    def picked(p, g, column):
        chosen, low = None, 0
        for q in range(p + 1):
            tiles = knowns[q][g].shape[0] // per_tile
            found = known_tile(q, g, jnp.clip(column - low, 0, tiles - 1))
            if chosen is None:
                chosen = found
            else:
                chosen = [jnp.where(column >= low, new, old) for new, old in zip(found, chosen)]
            low += tiles
        return chosen

    panel_tiles = n * share // tile
    first_tile = me * share // tile
    row_groups = range(share // rows_of)

    def slot_update(p, j, k, parts):
        update = jnp.zeros((part, rows_of), jnp.float32)
        for h in range(per_tile):
            update += lax.dot_general(
                parts[h],
                factor[p, k, j * rows_of : (j + 1) * rows_of, h * width : (h + 1) * width],
                NT,
                preferred_element_type=jnp.float32,
            )
        return update

    def residual_phase(p, g):
        early = None
        if share >= tile:
            early = [slot_update(p, j, 0, known_tile(p, g, first_tile + j)) for j in row_groups]

        wait_known(known_recv, p, g)
        for j in row_groups:
            row_tile = first_tile + j
            update = early[j] if early else slot_update(p, j, 0, known_tile(p, g, row_tile))
            opposite = lax.rem(row_tile + panel_tiles // 2, panel_tiles)
            update += slot_update(p, j, 1, known_tile(p, g, opposite))
            for k in range(2, factor.shape[1]):
                update += slot_update(p, j, k, picked(p, g, columns_ref[k, p, row_tile]))
            span = slice(j * rows_of, (j + 1) * rows_of)
            held = ordered[p, g * part : (g + 1) * part, span]
            residuals[p, g, me, :, span] = (held - update).astype(jnp.bfloat16)

        @pl.loop(0, n - 1 - me)
        def _(k):
            residual_copy(p, g, me, n - 1 - k).start()

    def product_phase(p, g):
        def product(src):
            return lax.dot_general(
                residuals[p, g, src],
                inverse[p, :, pl.ds(pl.multiple_of(src * share, share), share)],
                NT,
                preferred_element_type=jnp.float32,
            )

        total[...] = product(me)

        @pl.loop(1, me + 1)
        def _(d):
            src = me - d
            residual_copy(p, g, src, me).wait_recv()
            total[...] += product(src)

        solved = total[...]
        if p < panels - 1:
            for h in range(pieces):
                knowns[p + 1][g][me * pieces + h] = solved[:, h * width : (h + 1) * width].astype(
                    jnp.bfloat16
                )
            send_known(p + 1, g)
        out_ref[p, g] = solved
        pltpu.make_async_copy(
            out_ref.at[p, g], out_hbm.at[p, mocks_of(g)], out_sem.at[p, g]
        ).start()

    for p in range(panels):
        factor_copies[p].wait()
        for g in range(groups):
            residual_phase(p, g)
        if p + 1 < panels:
            gather(p + 1)
        inverse_copies[p].wait()
        for g in range(groups):
            product_phase(p, g)

    for p in range(panels):
        for g in range(groups):
            wait_known(known_send, p, g)
            pltpu.make_async_copy(
                out_ref.at[p, g], out_hbm.at[p, mocks_of(g)], out_sem.at[p, g]
            ).wait()

            @pl.loop(0, n - 1 - me)
            def _(k):
                residual_copy(p, g, me, n - 1 - k).wait_send()


def per_device(n, mock_maps, pixel_order, prior_solution, factor_rows, tile_columns, panel_inverse):
    mocks, panels, share = mock_maps.shape
    slots, tile = factor_rows.shape[2:]
    width = min(share, tile, prior_solution.shape[1])
    prior_pieces = prior_solution.shape[1] // width
    groups = GROUPS
    part = mocks // groups
    factor_slots = jnp.transpose(factor_rows, (0, 2, 1, 3))
    columns = jnp.transpose(tile_columns, (2, 0, 1))
    known_pieces = [n * prior_pieces] + [n * share // width] * (panels - 1)
    any_spec = pl.BlockSpec(memory_space=pl.ANY)
    dma = pltpu.SemaphoreType.DMA
    out = pl.pallas_call(
        functools.partial(solve_kernel, n, tile),
        out_shape=jax.ShapeDtypeStruct((panels, mocks, share), jnp.float32),
        in_specs=[
            pl.BlockSpec(memory_space=pltpu.SMEM), any_spec, any_spec,
            any_spec, any_spec, any_spec,
        ],
        out_specs=any_spec,
        scratch_shapes=[
            pltpu.VMEM(pixel_order.shape, jnp.int32),
            pltpu.VMEM(mock_maps.shape, jnp.float32),
            pltpu.VMEM((panels, groups, part, share), jnp.float32),
            dma((2,)),
            dma((panels, groups)),
            pltpu.VMEM((panels, groups, n, part, share), jnp.bfloat16),
            pltpu.VMEM(panel_inverse.shape, jnp.bfloat16),
            pltpu.VMEM(factor_slots.shape, jnp.bfloat16),
            pltpu.VMEM((panels, mocks, share), jnp.float32),
            pltpu.VMEM((part, share), jnp.float32),
            dma((groups, prior_pieces)),
            dma((panels,)),
            dma((panels,)),
            dma((panels, groups)),
            dma((panels, groups)),
            dma((panels, groups, n)),
            dma((panels, groups, n)),
        ]
        + [
            pltpu.VMEM((count, part, width), jnp.bfloat16)
            for count in known_pieces
            for _ in range(groups)
        ],
        compiler_params=pltpu.CompilerParams(
            collective_id=0, has_side_effects=True, vmem_limit_bytes=60 * 1024 * 1024
        ),
    )(columns, pixel_order, mock_maps, prior_solution, factor_slots, panel_inverse)
    return jnp.transpose(out, (1, 0, 2))


def solution(mesh):
    return jax.shard_map(
        functools.partial(per_device, mesh.shape["row"]),
        mesh=mesh,
        in_specs=(
            P("mock", None, "row"),
            P(None, "row"),
            P("mock", "row"),
            P(None, "row", None, None),
            P(),
            P(None, "row", None),
        ),
        out_specs=P("mock", None, "row"),
        check_vma=False,
    )
```

time: 63.1 us -> 59.5 us (0.943)
  the two profiles are of different devices: /device:TPU:8 before, /device:TPU:12 now
where the time goes in v1:
time: 59.5 us; the launch traced here: 59.3 us
  Pallas kernels  57.5 us (97%)
  local copies, waits for them, and re-layouts  1.82 us (3%)
    pallas_call x1, Pallas kernels, per_device(): pl.pallas_call(functools.partial(solve_kernel, n, tile), out_shape=jax.Sh...  57.5 us
    transpose x1, local copies, waits for them, and re-layouts, per_device(): return jnp.transpose(out, (1, 0, 2))  1.82 us

profile of v1, /device:TPU:12, one launch (start us, length us, event | category | flops | bytes accessed | tf_op | source)
XLA Modules:
  0.0 59.3 jit_solution(8089209183771262248)
XLA Ops:
  0.0 57.5 %shard_map.64 = f32[4,32,512]{2,1,0:T(8,128)} custom-call(s32[3,4,16]{2,1,0:T(4,128)} %bitcast.5, s32[4,512]{1,0:T(4,128)} %order_hbm.1, f32[32,4,512]{2,1,0:T(4,128)} %maps_hbm.1, bf16[32,512]{1,0:T(8,128)(2,1)} %prior_hbm.1, bf16[4,3,512,256]{3,2,1,0:T(8,128)(2,1)} %bitcast.3, bf16[4,512,4096]{2,1,0:T(8,128)(2,1)} %inverse_hbm.1), custom_call_target="tpu_custom_call" | custom-call | tf_op jit(solution)/shard_map/pallas_call | solution.py:241
  57.5 1.8 %copy.7 = f32[32,4,512]{2,1,0:T(4,128)} copy(f32[32,4,512]{2,0,1:T(8,128)} %bitcast.4) | data formatting | bytes 524288 | tf_op jit(solution)/shard_map/transpose | solution.py:277
